TPU v7x, 32 devices: a whole 2x2x4 slice. The times are simulated.
32 devices in a mesh: face: 4 (over x, core), tile: 8 (over z, y).
Axes of the slice: x: 2, y: 2, z: 4, core: 2. Of those that a mesh axis runs over, the one named last changes fastest.
Arguments:
- field_in: bfloat16 [12, 48, 256, 256], P('face', None, 'tile'), may hold values from -6 to 6
- out_grad: bfloat16 [12, 48, 256, 256], P('face', None, 'tile'), may hold values from -6 to 6
- weight_first: bfloat16 [48, 48, 3, 3], replicated, may hold values from -0.3125 to 0.3125
- bias_first: float32 [48], replicated, may hold values from -3 to 3
- weight_second: bfloat16 [48, 48, 3, 3], replicated, may hold values from -0.3125 to 0.3125
- bias_second: float32 [48], replicated, may hold values from -3 to 3
- face_links: int32 [12, 4, 3], replicated, may hold values from 0 to 11, as said below
- corner_rules: int32 [12, 4], replicated, may hold values from 0 to 1
Outputs:
- output_field: bfloat16 [12, 48, 256, 256], P('face', None, 'tile')
- grad_field: bfloat16 [12, 48, 256, 256], P('face', None, 'tile')
- grad_weight_first: float32 [48, 48, 3, 3], replicated
- grad_bias_first: float32 [48], replicated
- grad_weight_second: float32 [48, 48, 3, 3], replicated
- grad_bias_second: float32 [48], replicated
Inputs may be any that keep to these rules, and one draw needn't show every extreme that they name: face_links[f, e] = (g, e2, r) glues edge e of face f to edge e2 of face g; r = 1 when positions along the two edges run in opposite directions. The gluing is a pairing: (g, e2) differs from (f, e) and face_links[g, e2] = (f, e, r). The partner face lies in 0..11, the edge in 0..3, the flag in 0..1.
All inputs are finite; a program needn't handle non-finite values.
Results may differ from a plain program's by a relative error of at most 0.0055.
The roundings to bfloat16 on the way count: a program that leaves them out, or rounds other values in their place, can miss the bound.
Values may be sent and summed in bfloat16 or wider, within the bound.
A program may use at most 256 MiB of HBM per device.

v0:
```python
import jax
import jax.numpy as jnp
from jax import lax
from jax.sharding import PartitionSpec as P

INV_ROOT_TWO = 0.7071067811865476
INV_ROOT_TWO_PI = 0.3989422804014327


def shortened(x):
    return jax.tree.map(lambda a: a.astype(jnp.bfloat16) if a.dtype == jnp.float32 else a, x)


def extended_2(block, sides, width):
    for axis, dim in sides:
        count = lax.axis_size(axis)
        forward = [(i, i + 1) for i in range(count - 1)]
        backward = [(target, source) for source, target in forward]
        low = lax.ppermute(
            lax.slice_in_dim(block, block.shape[dim] - width, None, axis=dim), axis, forward
        )
        high = lax.ppermute(lax.slice_in_dim(block, 0, width, axis=dim), axis, backward)
        block = jnp.concatenate([low, block, high], axis=dim)
    return block


def gelu_pair(values):
    normal_cdf = 0.5 * (1.0 + lax.erf(values * INV_ROOT_TWO))
    normal_pdf = jnp.exp(-0.5 * values * values) * INV_ROOT_TWO_PI
    return (values * normal_cdf, normal_cdf + values * normal_pdf)


def convolve(padded, weight):
    return lax.conv_general_dilated(
        padded,
        weight,
        (1, 1),
        "VALID",
        dimension_numbers=("NCHW", "OIHW", "NCHW"),
        preferred_element_type=jnp.float32,
    )


def halo_rows(strip):
    return extended_2(shortened(strip), (("tile", 2),), 1).astype(strip.dtype)


def place_lines(north_row, south_row, west_part, east_part, tile_pos, tile_count):
    seg_len = west_part.shape[-1]
    mirrored = tile_count - 1 - tile_pos
    blanks = jnp.zeros(north_row.shape, jnp.float32)
    north_full = jnp.where(tile_pos == 0, north_row.astype(jnp.float32), blanks)
    south_full = jnp.where(tile_pos == tile_count - 1, south_row.astype(jnp.float32), blanks)
    west_wide = west_part.astype(jnp.float32)
    east_wide = east_part.astype(jnp.float32)
    west_full = lax.dynamic_update_slice_in_dim(blanks, west_wide, tile_pos * seg_len, 2)
    east_full = lax.dynamic_update_slice_in_dim(blanks, east_wide, tile_pos * seg_len, 2)
    placed = jnp.stack([north_full, south_full, west_full, east_full], axis=1)
    own_lines = lax.psum(placed.astype(jnp.bfloat16), "tile")
    front = lax.dynamic_slice_in_dim(own_lines, tile_pos * seg_len, seg_len, 3)
    back = lax.dynamic_slice_in_dim(own_lines, mirrored * seg_len, seg_len, 3)
    return (front, back)


def partner_pieces(front, my_links, tile_pos, tile_count):
    faces_dev, _, channels, seg_len = front.shape
    side_len = seg_len * tile_count
    partner_face = my_links[:, :, 0].reshape(-1)
    partner_edge = my_links[:, :, 1].reshape(-1)
    flip_mask = (my_links[:, :, 2] == 1).reshape(-1)
    gathered = lax.all_gather(front, ("face", "tile"), axis=3, tiled=True)

    def fetch_line(face_id, edge_id):
        start = (face_id % faces_dev, edge_id, 0, face_id // faces_dev * side_len)
        return lax.dynamic_slice(gathered, start, (1, 1, channels, side_len))[0, 0]

    source = jax.vmap(fetch_line)(partner_face, partner_edge)
    ghosts = jnp.where(flip_mask[:, None, None], source[:, :, ::-1], source)
    ghosts = ghosts.reshape(faces_dev, 4, channels, side_len)
    north_row = ghosts[:, 0]
    south_row = ghosts[:, 1]
    west_part = lax.dynamic_slice_in_dim(ghosts[:, 2], tile_pos * seg_len, seg_len, 2)
    east_part = lax.dynamic_slice_in_dim(ghosts[:, 3], tile_pos * seg_len, seg_len, 2)
    return (north_row, south_row, west_part, east_part)


def fill_strip(activation, my_links, my_corners, tile_pos, tile_count):
    front, back = place_lines(
        activation[:, :, 0, :],
        activation[:, :, -1, :],
        activation[:, :, :, 0],
        activation[:, :, :, -1],
        tile_pos,
        tile_count,
    )
    north_row, south_row, west_part, east_part = partner_pieces(
        front, my_links, tile_pos, tile_count
    )
    corner_code = (my_corners == 0)[:, :, None]
    corner_nw = jnp.where(corner_code[:, 0], north_row[:, :, 0], west_part[:, :, 0])
    corner_ne = jnp.where(corner_code[:, 1], north_row[:, :, -1], east_part[:, :, 0])
    corner_sw = jnp.where(corner_code[:, 2], south_row[:, :, 0], west_part[:, :, -1])
    corner_se = jnp.where(corner_code[:, 3], south_row[:, :, -1], east_part[:, :, -1])
    middle = jnp.concatenate(
        [west_part[:, :, :, None], activation, east_part[:, :, :, None]], axis=3
    )
    extended = halo_rows(middle)
    top_row = jnp.concatenate([corner_nw[:, :, None], north_row, corner_ne[:, :, None]], axis=2)
    bottom_row = jnp.concatenate([corner_sw[:, :, None], south_row, corner_se[:, :, None]], axis=2)
    top_rim = jnp.where(tile_pos == 0, top_row, extended[:, :, 0])
    bottom_rim = jnp.where(tile_pos == tile_count - 1, bottom_row, extended[:, :, -1])
    return jnp.concatenate(
        [top_rim[:, :, None], extended[:, :, 1:-1], bottom_rim[:, :, None]], axis=2
    )


def unfold_strip(cotangent, weight, my_links, my_corners, tile_pos, tile_count):
    widened = jnp.pad(cotangent, ((0, 0), (0, 0), (0, 0), (1, 1)))
    extended = halo_rows(widened)
    padded = jnp.pad(extended, ((0, 0), (0, 0), (1, 1), (1, 1)))
    flipped = jnp.transpose(weight[:, :, ::-1, ::-1], (1, 0, 2, 3))
    pad_grad = convolve(padded, flipped)
    at_top = tile_pos == 0
    at_bottom = tile_pos == tile_count - 1
    north_row = pad_grad[:, :, 0, 1:-1]
    south_row = pad_grad[:, :, -1, 1:-1]
    west_part = pad_grad[:, :, 1:-1, 0]
    east_part = pad_grad[:, :, 1:-1, -1]
    corner_nw = pad_grad[:, :, 0, 0]
    corner_ne = pad_grad[:, :, 0, -1]
    corner_sw = pad_grad[:, :, -1, 0]
    corner_se = pad_grad[:, :, -1, -1]
    corner_code = my_corners[:, :, None]
    north_row = north_row.at[:, :, 0].add(jnp.where(corner_code[:, 0] == 0, corner_nw, 0.0))
    north_row = north_row.at[:, :, -1].add(jnp.where(corner_code[:, 1] == 0, corner_ne, 0.0))
    south_row = south_row.at[:, :, 0].add(jnp.where(corner_code[:, 2] == 0, corner_sw, 0.0))
    south_row = south_row.at[:, :, -1].add(jnp.where(corner_code[:, 3] == 0, corner_se, 0.0))
    west_part = west_part.at[:, :, 0].add(
        jnp.where((corner_code[:, 0] == 1) & at_top, corner_nw, 0.0)
    )
    west_part = west_part.at[:, :, -1].add(
        jnp.where((corner_code[:, 2] == 1) & at_bottom, corner_sw, 0.0)
    )
    east_part = east_part.at[:, :, 0].add(
        jnp.where((corner_code[:, 1] == 1) & at_top, corner_ne, 0.0)
    )
    east_part = east_part.at[:, :, -1].add(
        jnp.where((corner_code[:, 3] == 1) & at_bottom, corner_se, 0.0)
    )
    front, back = place_lines(
        north_row.astype(jnp.bfloat16),
        south_row.astype(jnp.bfloat16),
        west_part.astype(jnp.bfloat16),
        east_part.astype(jnp.bfloat16),
        tile_pos,
        tile_count,
    )
    back_north, back_south, back_west, back_east = partner_pieces(
        front, my_links, tile_pos, tile_count
    )
    interior = pad_grad[:, :, 1:-1, 1:-1]
    interior = interior.at[:, :, 0, :].add(jnp.where(at_top, back_north.astype(jnp.float32), 0.0))
    interior = interior.at[:, :, -1, :].add(
        jnp.where(at_bottom, back_south.astype(jnp.float32), 0.0)
    )
    interior = interior.at[:, :, :, 0].add(back_west.astype(jnp.float32))
    interior = interior.at[:, :, :, -1].add(back_east.astype(jnp.float32))
    return interior


def weight_grad(cotangent, padded):
    return lax.conv_general_dilated(
        padded,
        cotangent,
        (1, 1),
        "VALID",
        dimension_numbers=("CNHW", "IOHW", "CNHW"),
        preferred_element_type=jnp.float32,
    )


def body(
    field_in,
    out_grad,
    weight_first,
    bias_first,
    weight_second,
    bias_second,
    face_links,
    corner_rules,
):
    tile_count = lax.axis_size("tile")
    tile_pos = lax.axis_index("tile")
    face_pos = lax.axis_index("face")
    faces_dev = field_in.shape[0]
    side_len = field_in.shape[3]
    my_links = lax.dynamic_slice_in_dim(face_links, face_pos * faces_dev, faces_dev, 0)
    my_corners = lax.dynamic_slice_in_dim(corner_rules, face_pos * faces_dev, faces_dev, 0)
    padded_first = fill_strip(field_in, my_links, my_corners, tile_pos, tile_count)
    pre_first = convolve(padded_first, weight_first) + bias_first[None, :, None, None]
    gelu_first, slope_first = gelu_pair(pre_first)
    hidden = gelu_first.astype(jnp.bfloat16)
    padded_second = fill_strip(hidden, my_links, my_corners, tile_pos, tile_count)
    pre_second = convolve(padded_second, weight_second) + bias_second[None, :, None, None]
    gelu_second, slope_second = gelu_pair(pre_second)
    output_field = gelu_second.astype(jnp.bfloat16)
    grad_second = (out_grad.astype(jnp.float32) * slope_second).astype(jnp.bfloat16)
    weight_second_part = weight_grad(grad_second, padded_second)
    bias_second_part = jnp.sum(grad_second.astype(jnp.float32), axis=(0, 2, 3))
    grad_hidden = unfold_strip(
        grad_second, weight_second, my_links, my_corners, tile_pos, tile_count
    )
    grad_first = (grad_hidden * slope_first).astype(jnp.bfloat16)
    weight_first_part = weight_grad(grad_first, padded_first)
    bias_first_part = jnp.sum(grad_first.astype(jnp.float32), axis=(0, 2, 3))
    grad_field = unfold_strip(
        grad_first, weight_first, my_links, my_corners, tile_pos, tile_count
    ).astype(jnp.bfloat16)
    totals = lax.psum(
        (weight_first_part, bias_first_part, weight_second_part, bias_second_part), ("face", "tile")
    )
    return (
        output_field,
        grad_field,
        totals[0] / side_len,
        totals[1] / side_len,
        totals[2] / side_len,
        totals[3] / side_len,
    )


def solution(mesh):
    return jax.shard_map(
        body,
        mesh=mesh,
        in_specs=(
            P("face", None, "tile", None),
            P("face", None, "tile", None),
            P(),
            P(),
            P(),
            P(),
            P(),
            P(),
        ),
        out_specs=(
            P("face", None, "tile", None),
            P("face", None, "tile", None),
            P(),
            P(),
            P(),
            P(),
        ),
        check_vma=False,
    )
```

profile of v0, /device:TPU:0, one launch (start us, length us, event | category | flops | bytes accessed | tf_op | source)
XLA Modules:
  0.0 1963.4 jit_solution(1567796698921269111)
XLA Ops:
  19.2 74.5 %all-reduce.10.cloned.1.call-done = bf16[3,4,48,256]{3,2,0,1:T(8,128)(2,1)} async-done(((bf16[3,4,48,256]{3,2,0,1:T(8,128)(2,1)}), bf16[3,4,48,256]{3,2,0,1:T(8,128)(2,1)}) %all-reduce.10.cloned.1.call-update) | async-done | bytes 294928 | tf_op jit(solution)/shard_map/psum | solution.py:59
  103.9 51.9 %all-gather.5.cloned.1.call-done = bf16[3,4,48,1024]{2,1,0,3:T(4,128)(2,1)} async-done(((bf16[3,4,48,32]{2,1,0,3:T(4,128)(2,1)}), bf16[3,4,48,1024]{2,1,0,3:T(4,128)(2,1)}) %all-gather.5.cloned.1.call-update) | async-done | bytes 1179664 | tf_op jit(solution)/shard_map/all_gather | solution.py:71
  179.5 17.8 fusion.87
  203.9 24.2 %copy.2867 = bf16[48,34,3,8,33]{4,3,0,2,1:T(8,128)(2,1)} copy(bf16[48,34,3,8,33]{0,2,4,3,1:T(4,128)(2,1)} %bitcast.324) | data formatting | bytes 5170176 | tf_op jit(solution)/shard_map/conv_general_dilated | solution.py:34
  268.8 23.4 %fusion.8 = (f32[32,24,33,48]{3,1,2,0:T(8,128)}, bf16[32,24,33,48]{3,1,2,0:T(8,128)(2,1)S(1)}) fusion(f32[48]{0:T(128)S(1)} %copy-done.49, pred[24,33]{0,1:T(8,128)(4,1)S(1)} %copy-done.53, bf16[48,48,3,3]{1,0,3,2:T(8,128)(2,1)S(1)} %copy-done.47, bf16[48,34,3,8,35]{0,3,2,4,1:T(8,128)(2,1)} %copy.2762), kind=kOutput, calls=%fused_computation.21 | convolution fusion | flops 1065664512 | bytes 10083288 | tf_op jit(solution)/shard_map/conv_general_dilated | solution.py:34
  311.7 72.1 %all-reduce.12.cloned.1.call-done = bf16[3,4,48,256]{3,2,0,1:T(8,128)(2,1)} async-done(((bf16[3,4,48,256]{3,2,0,1:T(8,128)(2,1)}), bf16[3,4,48,256]{3,2,0,1:T(8,128)(2,1)}) %all-reduce.12.cloned.1.call-update) | async-done | bytes 294928 | tf_op jit(solution)/shard_map/psum | solution.py:59
  386.0 59.4 %all-gather.7.cloned.1.call-done = bf16[3,4,48,1024]{2,1,0,3:T(4,128)(2,1)} async-done(((bf16[3,4,48,32]{2,1,0,3:T(4,128)(2,1)}), bf16[3,4,48,1024]{2,1,0,3:T(4,128)(2,1)}) %all-gather.7.cloned.1.call-update) | async-done | bytes 1179664 | tf_op jit(solution)/shard_map/all_gather | solution.py:71
  468.6 19.1 fusion.84
  494.3 24.2 %copy.2872 = bf16[48,34,3,8,33]{4,3,0,2,1:T(8,128)(2,1)} copy(bf16[48,34,3,8,33]{0,2,4,3,1:T(4,128)(2,1)} %bitcast.325) | data formatting | bytes 5170176 | tf_op jit(solution)/shard_map/conv_general_dilated | solution.py:34
  559.2 22.5 %fusion.12 = (f32[32,24,33,48]{3,1,2,0:T(8,128)}, bf16[32,24,33,48]{3,1,2,0:T(8,128)(2,1)}) fusion(f32[48]{0:T(128)S(1)} %copy-done.50, pred[24,33]{0,1:T(8,128)(4,1)S(1)} %copy-done.53, bf16[48,48,3,3]{1,0,3,2:T(8,128)(2,1)S(1)} %copy-done, bf16[48,34,3,8,35]{0,3,2,4,1:T(8,128)(2,1)} %copy.2782), kind=kOutput, calls=%fused_computation.25 | convolution fusion | flops 1065664512 | bytes 10083288 | tf_op jit(solution)/shard_map/conv_general_dilated | solution.py:34
  694.7 22.0 %convolution_select_fusion.1 = f32[34,24,33,48]{3,1,2,0:T(8,128)} fusion(bf16[48,48,3,3]{1,0,3,2:T(8,128)(2,1)S(1)} %copy-done, bf16[48,34,3,8,35]{0,3,2,4,1:T(8,128)(2,1)} %copy.2790, pred[24,33]{0,1:T(8,128)(4,1)S(1)} %copy-done.51), kind=kOutput, calls=%fused_computation.37 | convolution fusion | flops 1096153344 | bytes 7954200 | tf_op jit(solution)/shard_map/conv_general_dilated | solution.py:34
  746.0 17.6 copy.2888
  763.6 29.2 %fusion.67 = (f32[3,48,1,256]{2,1,0,3:T(8,128)}, f32[3,48,1,256]{2,1,0,3:T(8,128)}) fusion(f32[3,48,34,258]{2,1,0,3:T(8,128)} %bitcast.309), kind=kLoop, calls=%fused_computation.219 | loop fusion | bytes 589824 | tf_op jit(solution)/shard_map/slice | solution.py:125
  827.4 73.5 %all-reduce.14.cloned.1.call-done = bf16[3,4,48,256]{3,2,0,1:T(8,128)(2,1)} async-done(((bf16[3,4,48,256]{3,2,0,1:T(8,128)(2,1)}), bf16[3,4,48,256]{3,2,0,1:T(8,128)(2,1)}) %all-reduce.14.cloned.1.call-update) | async-done | bytes 294928 | tf_op jit(solution)/shard_map/psum | solution.py:59
  982.4 20.5 %slice_add_fusion.3 = f32[3,48,1,256]{2,1,0,3:T(8,128)} fusion(f32[3,48,1,256]{2,1,0,3:T(8,128)} %copy.2815, f32[3,48,34,258]{2,1,0,3:T(8,128)} %bitcast.315), kind=kLoop, calls=%fused_computation.14 | loop fusion | flops 36864 | bytes 442368 | tf_op jit(solution)/shard_map/add | solution.py:162
  1015.1 43.6 %scatter-add.94 = f32[3,48,32,256]{2,1,0,3:T(8,128)} dynamic-update-slice(f32[3,48,32,256]{2,1,0,3:T(8,128)} %slice.1002, f32[3,48,1,256]{2,1,0,3:T(8,128)} %slice_add_fusion.3, s32[]{:T(128)} %constant.616.clone.1, s32[]{:T(128)} %constant.616.clone.1, s32[]{:T(128)} %constant.616.clone.1, s32[]{:T(128)} %constant.616.clone.1) | dynamic-update-slice | bytes 294916 | tf_op jit(solution)/shard_map/scatter-add | solution.py:162
  1058.7 20.5 %slice_add_fusion.2 = f32[3,48,1,256]{2,1,0,3:T(8,128)} fusion(f32[3,48,1,256]{2,1,0,3:T(8,128)} %copy.2817, f32[3,48,32,256]{2,1,0,3:T(8,128)} %scatter-add.94), kind=kLoop, calls=%fused_computation.13 | loop fusion | flops 36864 | bytes 442368 | tf_op jit(solution)/shard_map/add | solution.py:163
  1079.2 73.5 %scatter-add.95 = f32[3,48,32,256]{2,1,0,3:T(8,128)} dynamic-update-slice(f32[3,48,32,256]{2,1,0,3:T(8,128)} %scatter-add.94, f32[3,48,1,256]{2,1,0,3:T(8,128)} %slice_add_fusion.2, s32[]{:T(128)} %constant.616.clone.1, s32[]{:T(128)} %constant.616.clone.1, s32[]{:T(128)} %constant.635.clone.1, s32[]{:T(128)} %constant.616.clone.1) | dynamic-update-slice | bytes 294916 | tf_op jit(solution)/shard_map/scatter-add | solution.py:163
  1207.4 44.8 %fusion.75 = f32[48,48,3,3]{0,1,3,2:T(8,128)} fusion(bf16[3,48,32,256]{1,0,3,2:T(4,128)(2,1)} %copy.2858, bf16[3,48,1,258]{1,0,3,2:T(4,128)(2,1)S(1)} %copy-done.15, bf16[3,48,32,1]{1,0,3,2:T(4,128)(2,1)S(1)} %copy-done.23, bf16[3,48,32,256]{1,0,3,2:T(4,128)(2,1)} %bitcast.319, bf16[3,48,32,1]{1,0,3,2:T(4,128)(2,1)S(1)} %copy-done.21, ...), kind=kOutput, calls=%fused_computation.227 | convolution fusion | flops 1031847552 | bytes 4968576 | tf_op jit(solution)/shard_map/conv_general_dilated | solution.py:172
  1342.3 21.8 %convolution_select_fusion = f32[34,24,33,48]{3,1,2,0:T(8,128)} fusion(bf16[48,48,3,3]{1,0,3,2:T(8,128)(2,1)S(1)} %copy-done.48, bf16[48,34,3,8,35]{0,3,2,4,1:T(8,128)(2,1)} %copy.2828, pred[24,33]{0,1:T(8,128)(4,1)S(1)} %copy-done.52), kind=kOutput, calls=%fused_computation.36 | convolution fusion | flops 1096153344 | bytes 7954200 | tf_op jit(solution)/shard_map/conv_general_dilated | solution.py:34
  1393.4 17.6 copy.2892
  1411.0 29.3 %fusion.66 = (f32[3,48,1,256]{2,1,0,3:T(8,128)}, f32[3,48,1,256]{2,1,0,3:T(8,128)}) fusion(f32[3,48,34,258]{2,1,0,3:T(8,128)} %bitcast.302), kind=kLoop, calls=%fused_computation.218 | loop fusion | bytes 589824 | tf_op jit(solution)/shard_map/slice | solution.py:125
  1475.0 44.8 %fusion.74 = f32[48,48,3,3]{0,1,3,2:T(8,128)} fusion(bf16[3,48,32,256]{1,0,3,2:T(4,128)(2,1)} %copy.2857, bf16[3,48,1,258]{1,0,3,2:T(4,128)(2,1)S(1)} %copy-done.11, bf16[3,48,32,1]{1,0,3,2:T(4,128)(2,1)S(1)} %copy-done.19, bf16[3,48,32,256]{1,0,3,2:T(4,128)(2,1)} %copy.2758, bf16[3,48,32,1]{1,0,3,2:T(4,128)(2,1)S(1)} %copy-done.17, ...), kind=kOutput, calls=%fused_computation.226 | convolution fusion | flops 1031847552 | bytes 4968576 | tf_op jit(solution)/shard_map/conv_general_dilated | solution.py:172
  1520.1 28.0 %all-reduce.16.cloned.1.call-done = bf16[3,4,48,256]{3,2,0,1:T(8,128)(2,1)} async-done(((bf16[3,4,48,256]{3,2,0,1:T(8,128)(2,1)}), bf16[3,4,48,256]{3,2,0,1:T(8,128)(2,1)}) %all-reduce.16.cloned.1.call-update) | async-done | bytes 294928 | tf_op jit(solution)/shard_map/psum | solution.py:59
  1567.8 39.3 %all-reduce.2 = (f32[48]{0:T(128)S(1)}, f32[48]{0:T(128)S(1)}) all-reduce(f32[48]{0:T(128)S(1)} %copy-done.46, f32[48]{0:T(128)S(1)} %copy-done.45), channel_id=1, replica_groups=mesh['face'=4,'tile'=8] {'face','tile'}, use_global_device_ids=true, to_apply=%region_6.7 | all-reduce | flops 96 | bytes 768 | tf_op jit(solution)/shard_map/psum | solution.py:219
  1608.2 16.6 slice.1030
  1624.8 54.6 %all-reduce.18.cloned.1.call-done = (f32[48,48,3,3]{0,1,3,2:T(8,128)}, f32[48,48,3,3]{0,1,3,2:T(8,128)}) async-done(((f32[48,48,3,3]{0,1,3,2:T(8,128)}, f32[48,48,3,3]{0,1,3,2:T(8,128)}), (f32[48,48,3,3]{0,1,3,2:T(8,128)}, f32[48,48,3,3]{0,1,3,2:T(8,128)})) %all-reduce.18.cloned.1.call-update) | async-done | bytes 165904 | tf_op jit(solution)/shard_map/psum | solution.py:219
  1683.0 60.5 %all-gather.11.cloned.1.call-done = bf16[3,4,48,1024]{2,1,0,3:T(4,128)(2,1)} async-done(((bf16[3,4,48,32]{2,1,0,3:T(4,128)(2,1)}), bf16[3,4,48,1024]{2,1,0,3:T(4,128)(2,1)}) %all-gather.11.cloned.1.call-update) | async-done | bytes 1179664 | tf_op jit(solution)/shard_map/all_gather | solution.py:71
  1760.5 20.5 %slice_add_fusion.1 = f32[3,48,1,256]{2,1,0,3:T(8,128)} fusion(f32[3,48,1,256]{2,1,0,3:T(8,128)} %copy.2852, f32[3,48,34,258]{2,1,0,3:T(8,128)} %bitcast.308), kind=kLoop, calls=%fused_computation.12 | loop fusion | flops 36864 | bytes 442368 | tf_op jit(solution)/shard_map/add | solution.py:162
  1793.2 43.6 %scatter-add.114 = f32[3,48,32,256]{2,1,0,3:T(8,128)} dynamic-update-slice(f32[3,48,32,256]{2,1,0,3:T(8,128)} %slice.1030, f32[3,48,1,256]{2,1,0,3:T(8,128)} %slice_add_fusion.1, s32[]{:T(128)} %constant.616.clone.1, s32[]{:T(128)} %constant.616.clone.1, s32[]{:T(128)} %constant.616.clone.1, s32[]{:T(128)} %constant.616.clone.1) | dynamic-update-slice | bytes 294916 | tf_op jit(solution)/shard_map/scatter-add | solution.py:162
  1836.8 20.5 %slice_add_fusion = f32[3,48,1,256]{2,1,0,3:T(8,128)} fusion(f32[3,48,1,256]{2,1,0,3:T(8,128)} %copy.2854, f32[3,48,32,256]{2,1,0,3:T(8,128)} %scatter-add.114), kind=kLoop, calls=%fused_computation.11 | loop fusion | flops 36864 | bytes 442368 | tf_op jit(solution)/shard_map/add | solution.py:163
  1857.3 73.6 %scatter-add.115 = f32[3,48,32,256]{2,1,0,3:T(8,128)} dynamic-update-slice(f32[3,48,32,256]{2,1,0,3:T(8,128)} %scatter-add.114, f32[3,48,1,256]{2,1,0,3:T(8,128)} %slice_add_fusion, s32[]{:T(128)} %constant.616.clone.1, s32[]{:T(128)} %constant.616.clone.1, s32[]{:T(128)} %constant.635.clone.1, s32[]{:T(128)} %constant.616.clone.1) | dynamic-update-slice | bytes 294916 | tf_op jit(solution)/shard_map/scatter-add | solution.py:163
  (365 shorter events, 742.7 us)
Async XLA Ops:
  7.2 552.0 %copy-start = (bf16[48,48,3,3]{1,0,3,2:T(8,128)(2,1)S(1)}, bf16[48,48,3,3]{1,0,3,2:T(8,128)(2,1)}, u32[]{:S(2)}) copy-start(bf16[48,48,3,3]{1,0,3,2:T(8,128)(2,1)} %param.60) | copy-start | bytes 124420
  7.2 86.5 %all-reduce.10.cloned.1.call-start = ((), (), s32[]{:S(2)}) async-start(), calls=%async_computation | async-start | bytes 589824 | tf_op jit(solution)/shard_map/psum | solution.py:59
  7.2 95.1 %copy-start.24 = (s32[12,4,3]{0,1,2:T(4,128)S(1)}, s32[12,4,3]{0,1,2:T(4,128)}, u32[]{:S(2)}) copy-start(s32[12,4,3]{0,1,2:T(4,128)} %param.62) | copy-start | bytes 1732
  7.3 96.2 %copy-start.44 = (s32[12,4]{0,1:T(4,128)S(1)}, s32[12,4]{0,1:T(4,128)}, u32[]{:S(2)}) copy-start(s32[12,4]{0,1:T(4,128)} %param.63) | copy-start | bytes 580
  19.2 136.6 %all-gather.5.cloned.1.call-start = ((), (), s32[]{:S(2)}) async-start(), calls=%async_computation.1 | async-start | bytes 3244032 | tf_op jit(solution)/shard_map/all_gather | solution.py:71
  95.5 288.3 %all-reduce.12.cloned.1.call-start = ((), (), s32[]{:S(2)}) async-start(), calls=%async_computation.2 | async-start | bytes 589824 | tf_op jit(solution)/shard_map/psum | solution.py:59
  103.4 345.7 %copy-start.25 = (pred[12]{0:T(512)(128)(4,1)}, pred[12]{0:T(512)(128)(4,1)S(1)}, u32[]{:S(2)}) copy-start(pred[12]{0:T(512)(128)(4,1)S(1)} %eq.133) | copy-start | bytes 40
  103.9 341.5 %copy-start.5 = (s32[12]{0:T(128)}, s32[12]{0:T(128)S(1)}, u32[]{:S(2)}) copy-start(s32[12]{0:T(128)S(1)} %fusion.63) | copy-start | bytes 148
  163.5 15.4 collective-permute-start
  167.1 12.0 collective-permute-start.1
  311.7 133.7 %all-gather.7.cloned.1.call-start = ((), (), s32[]{:S(2)}) async-start(), calls=%async_computation.3 | async-start | bytes 3244032 | tf_op jit(solution)/shard_map/all_gather | solution.py:71
  385.6 515.3 %all-reduce.14.cloned.1.call-start = ((), (), s32[]{:S(2)}) async-start(), calls=%async_computation.4 | async-start | bytes 589824 | tf_op jit(solution)/shard_map/psum | solution.py:59
  452.9 15.1 collective-permute-start.2
  456.3 12.0 collective-permute-start.3
  621.4 13.5 collective-permute-start.4
  625.8 9.1 collective-permute-start.5
  627.4 192.8 %copy-start.38 = (pred[3]{0:T(512)(128)(4,1)}, pred[3]{0:T(512)(128)(4,1)S(1)}, u32[]{:S(2)}) copy-start(pred[3]{0:T(512)(128)(4,1)S(1)} %get-tuple-element.458) | copy-start | bytes 13
  627.4 192.8 %copy-start.40 = (pred[3]{0:T(512)(128)(4,1)}, pred[3]{0:T(512)(128)(4,1)S(1)}, u32[]{:S(2)}) copy-start(pred[3]{0:T(512)(128)(4,1)S(1)} %get-tuple-element.462) | copy-start | bytes 13
  627.4 192.8 %copy-start.42 = (pred[3]{0:T(512)(128)(4,1)}, pred[3]{0:T(512)(128)(4,1)S(1)}, u32[]{:S(2)}) copy-start(pred[3]{0:T(512)(128)(4,1)S(1)} %get-tuple-element.463) | copy-start | bytes 13
  627.5 194.5 %copy-start.30 = (pred[3]{0:T(512)(128)(4,1)}, pred[3]{0:T(512)(128)(4,1)S(1)}, u32[]{:S(2)}) copy-start(pred[3]{0:T(512)(128)(4,1)S(1)} %get-tuple-element.456) | copy-start | bytes 13
  627.5 194.5 %copy-start.32 = (pred[3]{0:T(512)(128)(4,1)}, pred[3]{0:T(512)(128)(4,1)S(1)}, u32[]{:S(2)}) copy-start(pred[3]{0:T(512)(128)(4,1)S(1)} %get-tuple-element.457) | copy-start | bytes 13
  627.5 194.5 %copy-start.34 = (pred[3]{0:T(512)(128)(4,1)}, pred[3]{0:T(512)(128)(4,1)S(1)}, u32[]{:S(2)}) copy-start(pred[3]{0:T(512)(128)(4,1)S(1)} %get-tuple-element.460) | copy-start | bytes 13
  627.5 194.5 %copy-start.36 = (pred[3]{0:T(512)(128)(4,1)}, pred[3]{0:T(512)(128)(4,1)S(1)}, u32[]{:S(2)}) copy-start(pred[3]{0:T(512)(128)(4,1)S(1)} %get-tuple-element.461) | copy-start | bytes 13
  627.5 196.7 %copy-start.28 = (pred[3]{0:T(512)(128)(4,1)}, pred[3]{0:T(512)(128)(4,1)S(1)}, u32[]{:S(2)}) copy-start(pred[3]{0:T(512)(128)(4,1)S(1)} %get-tuple-element.459) | copy-start | bytes 13
  827.4 137.6 %all-gather.9.cloned.1.call-start = ((), (), s32[]{:S(2)}) async-start(), calls=%async_computation.5 | async-start | bytes 3244032 | tf_op jit(solution)/shard_map/all_gather | solution.py:71
  902.8 645.3 %all-reduce.16.cloned.1.call-start = ((), (), s32[]{:S(2)}) async-start(), calls=%async_computation.6 | async-start | bytes 589824 | tf_op jit(solution)/shard_map/psum | solution.py:59
  1191.2 90.2 %collective-permute-start.6 = (bf16[3,48,1,258]{3,1,2,0:T(8,128)(2,1)}, bf16[3,48,1,258]{3,1,2,0:T(8,128)(2,1)}, u32[]{:S(2)}, u32[]{:S(2)}) collective-permute-start(bf16[3,48,1,258]{3,1,2,0:T(8,128)(2,1)} %copy.2824), channel_id=1, source_target_pairs={{0,1},{1,2},{2,3},{3,4},{4,5},{5,6},{6,7},{8,9},{9,10},{10,11},{11... | collective-permute-start | bytes 222920 | tf_op jit(solution)/shard_map/ppermute | solution.py:19
  1206.1 75.3 %collective-permute-start.7 = (bf16[3,48,1,258]{3,1,2,0:T(8,128)(2,1)}, bf16[3,48,1,258]{3,1,2,0:T(8,128)(2,1)}, u32[]{:S(2)}, u32[]{:S(2)}) collective-permute-start(bf16[3,48,1,258]{3,1,2,0:T(8,128)(2,1)} %copy.2825), channel_id=1, source_target_pairs={{1,0},{2,1},{3,2},{4,3},{5,4},{6,5},{7,6},{9,8},{10,9},{11,10},{12... | collective-permute-start | bytes 222920 | tf_op jit(solution)/shard_map/ppermute | solution.py:22
  1474.9 204.5 %all-reduce.18.cloned.1.call-start = ((), (), s32[]{:S(2)}) async-start(), calls=%async_computation.8 | async-start | bytes 884736 | tf_op jit(solution)/shard_map/psum | solution.py:219
  1519.8 223.6 %all-gather.11.cloned.1.call-start = ((), (), s32[]{:S(2)}) async-start(), calls=%async_computation.7 | async-start | bytes 3244032 | tf_op jit(solution)/shard_map/all_gather | solution.py:71
  1608.2 135.2 %copy-start.7 = (s32[12]{0:T(128)S(1)}, s32[12]{0:T(128)}, u32[]{:S(2)}) copy-start(s32[12]{0:T(128)} %copy-done.5) | copy-start | bytes 148
  1608.2 139.0 %copy-start.27 = (pred[12]{0:T(512)(128)(4,1)S(1)}, pred[12]{0:T(512)(128)(4,1)}, u32[]{:S(2)}) copy-start(pred[12]{0:T(512)(128)(4,1)} %copy-done.25) | copy-start | bytes 40
  (39 other events, 895.6 us)
Sparse Core Ops, SparseCore 0:
  19.3 74.3 all-reduce.9
  97.6 58.1 all-gather.4
  311.8 71.9 all-reduce.11
  387.2 58.1 all-gather.6
  827.5 73.4 all-reduce.13
  904.7 58.1 all-gather.8
  1475.0 72.9 all-reduce.15
  1554.0 125.3 all-reduce.17
  1683.3 60.0 all-gather.10
where the time goes:
time: 1990 us; the launch traced here: 1960 us
  local copies, waits for them, and re-layouts  973 us (49%)
  waiting for transfers between devices  499 us (25%)
  other arithmetic  236 us (12%)
  matrix products  179 us (9%)
  blocking collectives  39.3 us (2%)
  starting transfers between devices  21.1 us (1%)
    psum x4, waiting for transfers between devices, place_lines(): own_lines = lax.psum(placed.astype(jnp.bfloat16), 'tile')  248 us
    conv_general_dilated x16, local copies, waits for them, and re-layouts, convolve(): lax.conv_general_dilated(padded, weight, (1, 1), 'VALID', dimension_numbe...  238 us
    all_gather x4, waiting for transfers between devices, partner_pieces(): gathered = lax.all_gather(front, ('face', 'tile'), axis=3, tiled=True)  172 us
    scatter-add x2, local copies, waits for them, and re-layouts, unfold_strip(): interior.at[:, :, -1, :]  147 us
    unnamed x128, local copies, waits for them, and re-layouts  125 us
    conv_general_dilated x4, matrix products, convolve(): lax.conv_general_dilated(padded, weight, (1, 1), 'VALID', dimension_numbe...  89.7 us
    conv_general_dilated x2, matrix products, weight_grad(): lax.conv_general_dilated(padded, cotangent, (1, 1), 'VALID', dimension_nu...  89.7 us
    scatter-add x2, local copies, waits for them, and re-layouts, unfold_strip(): interior.at[:, :, 0, :]  87.2 us
  transfers between devices with their start and end apart: 17, of which 11 were waited for; matrix products, arithmetic and copies ran while one was open for 13% of the time, Pallas kernels for 0%

commit v1 on v0

--- a/solution.py
+++ b/solution.py
@@ -216,9 +216,13 @@
     grad_field = unfold_strip(
         grad_first, weight_first, my_links, my_corners, tile_pos, tile_count
     ).astype(jnp.bfloat16)
-    totals = lax.psum(
-        (weight_first_part, bias_first_part, weight_second_part, bias_second_part), ("face", "tile")
-    )
+
+    def pack_loads(content):
+        for k0 in ("tile", "face"):
+            content = lax.psum(content, axis_name=k0)
+        return content
+
+    totals = pack_loads((weight_first_part, bias_first_part, weight_second_part, bias_second_part))
     return (
         output_field,
         grad_field,

time: 1990 us -> 1900 us (0.955)
  waiting for transfers between devices: 499 us -> 415 us
    psum x1 -> x2, waiting for transfers between devices: 54.6 us -> 0.02 us  [pack_loads(): content = lax.psum(content, axis_name=k0)]
    all_gather x4, waiting for transfers between devices: 172 us -> 143 us  [partner_pieces(): gathered = lax.all_gather(front, ('face', 'tile'), axis=3, tiled=True)]
    unnamed x128 -> x126, local copies, waits for them, and re-layouts: 125 us -> 125 us
  transfers between devices with their start and end apart: 17 -> 18, of which waited for: 11 -> 10; matrix products, arithmetic and copies ran while one was open for 13% -> 23% of each run, Pallas kernels for 0% -> 0%
where the time goes in v1:
time: 1900 us; the launch traced here: 1880 us
  local copies, waits for them, and re-layouts  979 us (52%)
  waiting for transfers between devices  415 us (22%)
  other arithmetic  240 us (13%)
  matrix products  180 us (9%)
  blocking collectives  25.3 us (1%)
  starting transfers between devices  21.2 us (1%)
    psum x4, waiting for transfers between devices, place_lines(): own_lines = lax.psum(placed.astype(jnp.bfloat16), 'tile')  247 us
    conv_general_dilated x16, local copies, waits for them, and re-layouts, convolve(): lax.conv_general_dilated(padded, weight, (1, 1), 'VALID', dimension_numbe...  238 us
    scatter-add x2, local copies, waits for them, and re-layouts, unfold_strip(): interior.at[:, :, -1, :]  147 us
    all_gather x4, waiting for transfers between devices, partner_pieces(): gathered = lax.all_gather(front, ('face', 'tile'), axis=3, tiled=True)  143 us
    unnamed x126, local copies, waits for them, and re-layouts  125 us
    conv_general_dilated x4, matrix products, convolve(): lax.conv_general_dilated(padded, weight, (1, 1), 'VALID', dimension_numbe...  90 us
    conv_general_dilated x2, matrix products, weight_grad(): lax.conv_general_dilated(padded, cotangent, (1, 1), 'VALID', dimension_nu...  89.8 us
    scatter-add x2, local copies, waits for them, and re-layouts, unfold_strip(): interior.at[:, :, 0, :]  87.2 us
  transfers between devices with their start and end apart: 18, of which 10 were waited for; matrix products, arithmetic and copies ran while one was open for 23% of the time, Pallas kernels for 0%

profile of v1, /device:TPU:0, one launch (start us, length us, event | category | flops | bytes accessed | tf_op | source)
XLA Modules:
  0.0 1876.3 jit_solution(5511332149891210849)
XLA Ops:
  19.2 74.5 %all-reduce.13.cloned.1.call-done = bf16[3,4,48,256]{3,2,0,1:T(8,128)(2,1)} async-done(((bf16[3,4,48,256]{3,2,0,1:T(8,128)(2,1)}), bf16[3,4,48,256]{3,2,0,1:T(8,128)(2,1)}) %all-reduce.13.cloned.1.call-update) | async-done | bytes 294928 | tf_op jit(solution)/shard_map/psum | solution.py:59
  103.9 51.9 %all-gather.5.cloned.1.call-done = bf16[3,4,48,1024]{2,1,0,3:T(4,128)(2,1)} async-done(((bf16[3,4,48,32]{2,1,0,3:T(4,128)(2,1)}), bf16[3,4,48,1024]{2,1,0,3:T(4,128)(2,1)}) %all-gather.5.cloned.1.call-update) | async-done | bytes 1179664 | tf_op jit(solution)/shard_map/all_gather | solution.py:71
  179.4 17.8 fusion.87
  203.9 24.2 %copy.2867 = bf16[48,34,3,8,33]{4,3,0,2,1:T(8,128)(2,1)} copy(bf16[48,34,3,8,33]{0,2,4,3,1:T(4,128)(2,1)} %bitcast.324) | data formatting | bytes 5170176 | tf_op jit(solution)/shard_map/conv_general_dilated | solution.py:34
  268.6 23.4 %fusion.8 = (f32[32,24,33,48]{3,1,2,0:T(8,128)}, bf16[32,24,33,48]{3,1,2,0:T(8,128)(2,1)S(1)}) fusion(f32[48]{0:T(128)S(1)} %copy-done.48, pred[24,33]{0,1:T(8,128)(4,1)S(1)} %copy-done.52, bf16[48,48,3,3]{1,0,3,2:T(8,128)(2,1)S(1)} %copy-done.46, bf16[48,34,3,8,35]{0,3,2,4,1:T(8,128)(2,1)} %copy.2762), kind=kOutput, calls=%fused_computation.21 | convolution fusion | flops 1065664512 | bytes 10083288 | tf_op jit(solution)/shard_map/conv_general_dilated | solution.py:34
  311.4 72.2 %all-reduce.15.cloned.1.call-done = bf16[3,4,48,256]{3,2,0,1:T(8,128)(2,1)} async-done(((bf16[3,4,48,256]{3,2,0,1:T(8,128)(2,1)}), bf16[3,4,48,256]{3,2,0,1:T(8,128)(2,1)}) %all-reduce.15.cloned.1.call-update) | async-done | bytes 294928 | tf_op jit(solution)/shard_map/psum | solution.py:59
  385.8 59.4 %all-gather.7.cloned.1.call-done = bf16[3,4,48,1024]{2,1,0,3:T(4,128)(2,1)} async-done(((bf16[3,4,48,32]{2,1,0,3:T(4,128)(2,1)}), bf16[3,4,48,1024]{2,1,0,3:T(4,128)(2,1)}) %all-gather.7.cloned.1.call-update) | async-done | bytes 1179664 | tf_op jit(solution)/shard_map/all_gather | solution.py:71
  468.3 19.1 %fusion.84 = bf16[48,34,3,258]{0,2,3,1:T(4,128)(2,1)S(1)} fusion(bf16[3,48,1,258]{1,0,3,2:T(4,128)(2,1)S(1)} %maximum_select_fusion.3, bf16[3,48,32,1]{1,0,3,2:T(4,128)(2,1)S(1)} %copy.2779, bf16[3,48,32,256]{1,0,3,2:T(4,128)(2,1)} %bitcast.318, bf16[3,48,32,1]{1,0,3,2:T(4,128)(2,1)S(1)} %copy.2778, bf16[3,48,1,258]{1,0,3,2:T(4,128)(2,1)S(1)} %maximum_select_fusion.2), kind=kLoop, calls=%fused_computation.228 | loop fusion | flops 5052672 | bytes 5052672 | tf_op jit(solution)/shard_map/concatenate | solution.py:112
  494.1 24.2 %copy.2872 = bf16[48,34,3,8,33]{4,3,0,2,1:T(8,128)(2,1)} copy(bf16[48,34,3,8,33]{0,2,4,3,1:T(4,128)(2,1)} %bitcast.325) | data formatting | bytes 5170176 | tf_op jit(solution)/shard_map/conv_general_dilated | solution.py:34
  558.8 22.5 %fusion.12 = (f32[32,24,33,48]{3,1,2,0:T(8,128)}, bf16[32,24,33,48]{3,1,2,0:T(8,128)(2,1)}) fusion(f32[48]{0:T(128)S(1)} %copy-done.49, pred[24,33]{0,1:T(8,128)(4,1)S(1)} %copy-done.52, bf16[48,48,3,3]{1,0,3,2:T(8,128)(2,1)S(1)} %copy-done, bf16[48,34,3,8,35]{0,3,2,4,1:T(8,128)(2,1)} %copy.2782), kind=kOutput, calls=%fused_computation.25 | convolution fusion | flops 1065664512 | bytes 10083288 | tf_op jit(solution)/shard_map/conv_general_dilated | solution.py:34
  694.0 22.1 %convolution_select_fusion.1 = f32[34,24,33,48]{3,1,2,0:T(8,128)} fusion(bf16[48,48,3,3]{1,0,3,2:T(8,128)(2,1)S(1)} %copy-done, bf16[48,34,3,8,35]{0,3,2,4,1:T(8,128)(2,1)} %copy.2790, pred[24,33]{0,1:T(8,128)(4,1)S(1)} %copy-done.50), kind=kOutput, calls=%fused_computation.37 | convolution fusion | flops 1096153344 | bytes 7954200 | tf_op jit(solution)/shard_map/conv_general_dilated | solution.py:34
  745.4 17.6 copy.2888
  763.1 28.9 %fusion.67 = (f32[3,48,1,256]{2,1,0,3:T(8,128)}, f32[3,48,1,256]{2,1,0,3:T(8,128)}) fusion(f32[3,48,34,258]{2,1,0,3:T(8,128)} %bitcast.309), kind=kLoop, calls=%fused_computation.219 | loop fusion | bytes 589824 | tf_op jit(solution)/shard_map/slice | solution.py:125
  872.2 28.1 %all-reduce.17.cloned.1.call-done = bf16[3,4,48,256]{3,2,0,1:T(8,128)(2,1)} async-done(((bf16[3,4,48,256]{3,2,0,1:T(8,128)(2,1)}), bf16[3,4,48,256]{3,2,0,1:T(8,128)(2,1)}) %all-reduce.17.cloned.1.call-update) | async-done | bytes 294928 | tf_op jit(solution)/shard_map/psum | solution.py:59
  902.1 45.0 %fusion.75 = f32[48,48,3,3]{0,1,3,2:T(8,128)} fusion(bf16[3,48,32,256]{1,0,3,2:T(4,128)(2,1)} %copy.2858, bf16[3,48,1,258]{1,0,3,2:T(4,128)(2,1)S(1)} %copy-done.14, bf16[3,48,32,1]{1,0,3,2:T(4,128)(2,1)S(1)} %copy-done.22, bf16[3,48,32,256]{1,0,3,2:T(4,128)(2,1)} %bitcast.319, bf16[3,48,32,1]{1,0,3,2:T(4,128)(2,1)S(1)} %copy-done.20, ...), kind=kOutput, calls=%fused_computation.227 | convolution fusion | flops 1031847552 | bytes 4968576 | tf_op jit(solution)/shard_map/conv_general_dilated | solution.py:172
  981.2 20.5 %slice_add_fusion.3 = f32[3,48,1,256]{2,1,0,3:T(8,128)} fusion(f32[3,48,1,256]{2,1,0,3:T(8,128)} %copy.2815, f32[3,48,34,258]{2,1,0,3:T(8,128)} %bitcast.315), kind=kLoop, calls=%fused_computation.14 | loop fusion | flops 36864 | bytes 442368 | tf_op jit(solution)/shard_map/add | solution.py:162
  1013.9 43.6 %scatter-add.94 = f32[3,48,32,256]{2,1,0,3:T(8,128)} dynamic-update-slice(f32[3,48,32,256]{2,1,0,3:T(8,128)} %slice.1002, f32[3,48,1,256]{2,1,0,3:T(8,128)} %slice_add_fusion.3, s32[]{:T(128)} %constant.616.clone.1, s32[]{:T(128)} %constant.616.clone.1, s32[]{:T(128)} %constant.616.clone.1, s32[]{:T(128)} %constant.616.clone.1) | dynamic-update-slice | bytes 294916 | tf_op jit(solution)/shard_map/scatter-add | solution.py:162
  1057.6 20.9 %slice_add_fusion.2 = f32[3,48,1,256]{2,1,0,3:T(8,128)} fusion(f32[3,48,1,256]{2,1,0,3:T(8,128)} %copy.2817, f32[3,48,32,256]{2,1,0,3:T(8,128)} %scatter-add.94), kind=kLoop, calls=%fused_computation.13 | loop fusion | flops 36864 | bytes 442368 | tf_op jit(solution)/shard_map/add | solution.py:163
  1078.5 73.6 %scatter-add.95 = f32[3,48,32,256]{2,1,0,3:T(8,128)} dynamic-update-slice(f32[3,48,32,256]{2,1,0,3:T(8,128)} %scatter-add.94, f32[3,48,1,256]{2,1,0,3:T(8,128)} %slice_add_fusion.2, s32[]{:T(128)} %constant.616.clone.1, s32[]{:T(128)} %constant.616.clone.1, s32[]{:T(128)} %constant.635.clone.1, s32[]{:T(128)} %constant.616.clone.1) | dynamic-update-slice | bytes 294916 | tf_op jit(solution)/shard_map/scatter-add | solution.py:163
  1155.2 17.1 convert_reduce_fusion
  1187.3 17.4 pad_slice_fusion.3
  1232.8 44.8 %fusion.74 = f32[48,48,3,3]{0,1,3,2:T(8,128)} fusion(bf16[3,48,32,256]{1,0,3,2:T(4,128)(2,1)} %copy.2857, bf16[3,48,1,258]{1,0,3,2:T(4,128)(2,1)S(1)} %copy-done.10, bf16[3,48,32,1]{1,0,3,2:T(4,128)(2,1)S(1)} %copy-done.18, bf16[3,48,32,256]{1,0,3,2:T(4,128)(2,1)} %copy.2758, bf16[3,48,32,1]{1,0,3,2:T(4,128)(2,1)S(1)} %copy-done.16, ...), kind=kOutput, calls=%fused_computation.226 | convolution fusion | flops 1031847552 | bytes 4968576 | tf_op jit(solution)/shard_map/conv_general_dilated | solution.py:172
  1352.8 21.9 %convolution_select_fusion = f32[34,24,33,48]{3,1,2,0:T(8,128)} fusion(bf16[48,48,3,3]{1,0,3,2:T(8,128)(2,1)S(1)} %copy-done.47, bf16[48,34,3,8,35]{0,3,2,4,1:T(8,128)(2,1)} %copy.2828, pred[24,33]{0,1:T(8,128)(4,1)S(1)} %copy-done.51), kind=kOutput, calls=%fused_computation.36 | convolution fusion | flops 1096153344 | bytes 7954200 | tf_op jit(solution)/shard_map/conv_general_dilated | solution.py:34
  1404.0 17.6 copy.2892
  1421.6 29.0 %fusion.66 = (f32[3,48,1,256]{2,1,0,3:T(8,128)}, f32[3,48,1,256]{2,1,0,3:T(8,128)}) fusion(f32[3,48,34,258]{2,1,0,3:T(8,128)} %bitcast.302), kind=kLoop, calls=%fused_computation.218 | loop fusion | bytes 589824 | tf_op jit(solution)/shard_map/slice | solution.py:125
  1486.0 72.4 %all-reduce.19.cloned.1.call-done = bf16[3,4,48,256]{3,2,0,1:T(8,128)(2,1)} async-done(((bf16[3,4,48,256]{3,2,0,1:T(8,128)(2,1)}), bf16[3,4,48,256]{3,2,0,1:T(8,128)(2,1)}) %all-reduce.19.cloned.1.call-update) | async-done | bytes 294928 | tf_op jit(solution)/shard_map/psum | solution.py:59
  1578.1 19.5 %all-reduce.2 = (f32[48]{0:T(128)S(1)}, f32[48]{0:T(128)S(1)}) all-reduce(f32[48]{0:T(128)S(1)} %copy-done.45, f32[48]{0:T(128)S(1)} %copy-done.44), channel_id=1, replica_groups=mesh['face'=4,'tile'=8] {'tile'}, use_global_device_ids=true, to_apply=%region_7.8 | all-reduce | flops 96 | bytes 768 | tf_op jit(solution)/shard_map/psum | solution.py:222
  1624.5 31.2 %all-gather.11.cloned.1.call-done = bf16[3,4,48,1024]{2,1,0,3:T(4,128)(2,1)} async-done(((bf16[3,4,48,32]{2,1,0,3:T(4,128)(2,1)}), bf16[3,4,48,1024]{2,1,0,3:T(4,128)(2,1)}) %all-gather.11.cloned.1.call-update) | async-done | bytes 1179664 | tf_op jit(solution)/shard_map/all_gather | solution.py:71
  1673.1 20.6 %slice_add_fusion.1 = f32[3,48,1,256]{2,1,0,3:T(8,128)} fusion(f32[3,48,1,256]{2,1,0,3:T(8,128)} %copy.2852, f32[3,48,34,258]{2,1,0,3:T(8,128)} %bitcast.308), kind=kLoop, calls=%fused_computation.12 | loop fusion | flops 36864 | bytes 442368 | tf_op jit(solution)/shard_map/add | solution.py:162
  1705.8 43.6 %scatter-add.114 = f32[3,48,32,256]{2,1,0,3:T(8,128)} dynamic-update-slice(f32[3,48,32,256]{2,1,0,3:T(8,128)} %slice.1030, f32[3,48,1,256]{2,1,0,3:T(8,128)} %slice_add_fusion.1, s32[]{:T(128)} %constant.616.clone.1, s32[]{:T(128)} %constant.616.clone.1, s32[]{:T(128)} %constant.616.clone.1, s32[]{:T(128)} %constant.616.clone.1) | dynamic-update-slice | bytes 294916 | tf_op jit(solution)/shard_map/scatter-add | solution.py:162
  1749.4 20.5 %slice_add_fusion = f32[3,48,1,256]{2,1,0,3:T(8,128)} fusion(f32[3,48,1,256]{2,1,0,3:T(8,128)} %copy.2854, f32[3,48,32,256]{2,1,0,3:T(8,128)} %scatter-add.114), kind=kLoop, calls=%fused_computation.11 | loop fusion | flops 36864 | bytes 442368 | tf_op jit(solution)/shard_map/add | solution.py:163
  1769.9 73.6 %scatter-add.115 = f32[3,48,32,256]{2,1,0,3:T(8,128)} dynamic-update-slice(f32[3,48,32,256]{2,1,0,3:T(8,128)} %scatter-add.114, f32[3,48,1,256]{2,1,0,3:T(8,128)} %slice_add_fusion, s32[]{:T(128)} %constant.616.clone.1, s32[]{:T(128)} %constant.616.clone.1, s32[]{:T(128)} %constant.635.clone.1, s32[]{:T(128)} %constant.616.clone.1) | dynamic-update-slice | bytes 294916 | tf_op jit(solution)/shard_map/scatter-add | solution.py:163
  (367 shorter events, 741.7 us)
Async XLA Ops:
  7.2 551.7 %copy-start = (bf16[48,48,3,3]{1,0,3,2:T(8,128)(2,1)S(1)}, bf16[48,48,3,3]{1,0,3,2:T(8,128)(2,1)}, u32[]{:S(2)}) copy-start(bf16[48,48,3,3]{1,0,3,2:T(8,128)(2,1)} %param.60) | copy-start | bytes 124420
  7.2 88.4 %copy-start.3 = (bf16[3,48,32,256]{3,2,1,0:T(8,128)(2,1)S(1)}, bf16[3,48,32,256]{3,2,1,0:T(8,128)(2,1)}, u32[]{:S(2)}) copy-start(bf16[3,48,32,256]{3,2,1,0:T(8,128)(2,1)} %param.56) | copy-start | bytes 7077892
  7.2 86.5 %all-reduce.13.cloned.1.call-start = ((), (), s32[]{:S(2)}) async-start(), calls=%async_computation | async-start | bytes 589824 | tf_op jit(solution)/shard_map/psum | solution.py:59
  7.2 95.1 %copy-start.23 = (s32[12,4,3]{0,1,2:T(4,128)S(1)}, s32[12,4,3]{0,1,2:T(4,128)}, u32[]{:S(2)}) copy-start(s32[12,4,3]{0,1,2:T(4,128)} %param.62) | copy-start | bytes 1732
  7.3 96.2 %copy-start.43 = (s32[12,4]{0,1:T(4,128)S(1)}, s32[12,4]{0,1:T(4,128)}, u32[]{:S(2)}) copy-start(s32[12,4]{0,1:T(4,128)} %param.63) | copy-start | bytes 580
  19.2 136.7 %all-gather.5.cloned.1.call-start = ((), (), s32[]{:S(2)}) async-start(), calls=%async_computation.1 | async-start | bytes 3244032 | tf_op jit(solution)/shard_map/all_gather | solution.py:71
  95.5 288.1 %all-reduce.15.cloned.1.call-start = ((), (), s32[]{:S(2)}) async-start(), calls=%async_computation.2 | async-start | bytes 589824 | tf_op jit(solution)/shard_map/psum | solution.py:59
  103.4 345.6 %copy-start.24 = (pred[12]{0:T(512)(128)(4,1)}, pred[12]{0:T(512)(128)(4,1)S(1)}, u32[]{:S(2)}) copy-start(pred[12]{0:T(512)(128)(4,1)S(1)} %eq.133) | copy-start | bytes 40
  103.9 341.3 %copy-start.4 = (s32[12]{0:T(128)}, s32[12]{0:T(128)S(1)}, u32[]{:S(2)}) copy-start(s32[12]{0:T(128)S(1)} %fusion.63) | copy-start | bytes 148
  163.6 15.3 collective-permute-start
  167.2 11.9 collective-permute-start.1
  311.4 133.8 %all-gather.7.cloned.1.call-start = ((), (), s32[]{:S(2)}) async-start(), calls=%async_computation.3 | async-start | bytes 3244032 | tf_op jit(solution)/shard_map/all_gather | solution.py:71
  385.4 514.8 %all-reduce.17.cloned.1.call-start = ((), (), s32[]{:S(2)}) async-start(), calls=%async_computation.4 | async-start | bytes 589824 | tf_op jit(solution)/shard_map/psum | solution.py:59
  452.8 15.0 collective-permute-start.2
  456.2 11.9 collective-permute-start.3
  620.9 13.4 collective-permute-start.4
  625.4 9.0 collective-permute-start.5
  627.0 192.5 %copy-start.37 = (pred[3]{0:T(512)(128)(4,1)}, pred[3]{0:T(512)(128)(4,1)S(1)}, u32[]{:S(2)}) copy-start(pred[3]{0:T(512)(128)(4,1)S(1)} %get-tuple-element.458) | copy-start | bytes 13
  627.0 192.5 %copy-start.39 = (pred[3]{0:T(512)(128)(4,1)}, pred[3]{0:T(512)(128)(4,1)S(1)}, u32[]{:S(2)}) copy-start(pred[3]{0:T(512)(128)(4,1)S(1)} %get-tuple-element.462) | copy-start | bytes 13
  627.0 192.5 %copy-start.41 = (pred[3]{0:T(512)(128)(4,1)}, pred[3]{0:T(512)(128)(4,1)S(1)}, u32[]{:S(2)}) copy-start(pred[3]{0:T(512)(128)(4,1)S(1)} %get-tuple-element.463) | copy-start | bytes 13
  627.0 194.2 %copy-start.29 = (pred[3]{0:T(512)(128)(4,1)}, pred[3]{0:T(512)(128)(4,1)S(1)}, u32[]{:S(2)}) copy-start(pred[3]{0:T(512)(128)(4,1)S(1)} %get-tuple-element.456) | copy-start | bytes 13
  627.0 194.2 %copy-start.31 = (pred[3]{0:T(512)(128)(4,1)}, pred[3]{0:T(512)(128)(4,1)S(1)}, u32[]{:S(2)}) copy-start(pred[3]{0:T(512)(128)(4,1)S(1)} %get-tuple-element.457) | copy-start | bytes 13
  627.0 194.2 %copy-start.33 = (pred[3]{0:T(512)(128)(4,1)}, pred[3]{0:T(512)(128)(4,1)S(1)}, u32[]{:S(2)}) copy-start(pred[3]{0:T(512)(128)(4,1)S(1)} %get-tuple-element.460) | copy-start | bytes 13
  627.0 194.2 %copy-start.35 = (pred[3]{0:T(512)(128)(4,1)}, pred[3]{0:T(512)(128)(4,1)S(1)}, u32[]{:S(2)}) copy-start(pred[3]{0:T(512)(128)(4,1)S(1)} %get-tuple-element.461) | copy-start | bytes 13
  627.0 196.3 %copy-start.27 = (pred[3]{0:T(512)(128)(4,1)}, pred[3]{0:T(512)(128)(4,1)S(1)}, u32[]{:S(2)}) copy-start(pred[3]{0:T(512)(128)(4,1)S(1)} %get-tuple-element.459) | copy-start | bytes 13
  826.5 137.1 %all-gather.9.cloned.1.call-start = ((), (), s32[]{:S(2)}) async-start(), calls=%async_computation.5 | async-start | bytes 3244032 | tf_op jit(solution)/shard_map/all_gather | solution.py:71
  902.1 583.2 %all-reduce.21.cloned.1.call-start = ((), (), s32[]{:S(2)}) async-start(), calls=%async_computation.8 | async-start | bytes 884736 | tf_op jit(solution)/shard_map/psum | solution.py:222
  1216.5 75.5 %collective-permute-start.6 = (bf16[3,48,1,258]{3,1,2,0:T(8,128)(2,1)}, bf16[3,48,1,258]{3,1,2,0:T(8,128)(2,1)}, u32[]{:S(2)}, u32[]{:S(2)}) collective-permute-start(bf16[3,48,1,258]{3,1,2,0:T(8,128)(2,1)} %copy.2824), channel_id=1, source_target_pairs={{0,1},{1,2},{2,3},{3,4},{4,5},{5,6},{6,7},{8,9},{9,10},{10,11},{11... | collective-permute-start | bytes 222920 | tf_op jit(solution)/shard_map/ppermute | solution.py:19
  1231.5 60.5 %collective-permute-start.7 = (bf16[3,48,1,258]{3,1,2,0:T(8,128)(2,1)}, bf16[3,48,1,258]{3,1,2,0:T(8,128)(2,1)}, u32[]{:S(2)}, u32[]{:S(2)}) collective-permute-start(bf16[3,48,1,258]{3,1,2,0:T(8,128)(2,1)} %copy.2825), channel_id=1, source_target_pairs={{1,0},{2,1},{3,2},{4,3},{5,4},{6,5},{7,6},{9,8},{10,9},{11,10},{12... | collective-permute-start | bytes 222920 | tf_op jit(solution)/shard_map/ppermute | solution.py:22
  1290.2 268.2 %all-reduce.19.cloned.1.call-start = ((), (), s32[]{:S(2)}) async-start(), calls=%async_computation.6 | async-start | bytes 589824 | tf_op jit(solution)/shard_map/psum | solution.py:59
  1485.2 135.7 %all-reduce.23.cloned.1.call-start = ((), (), s32[]{:S(2)}) async-start(), calls=%async_computation.9 | async-start | bytes 884736 | tf_op jit(solution)/shard_map/psum | solution.py:222
  1485.9 169.8 %all-gather.11.cloned.1.call-start = ((), (), s32[]{:S(2)}) async-start(), calls=%async_computation.7 | async-start | bytes 3244032 | tf_op jit(solution)/shard_map/all_gather | solution.py:71
  (39 other events, 970.8 us)
Sparse Core Ops, SparseCore 0:
  19.3 74.3 all-reduce.12
  97.6 58.2 all-gather.4
  311.5 72.1 all-reduce.14
  387.0 58.1 all-gather.6
  826.7 73.5 all-reduce.16
  904.0 58.1 all-gather.8
  1290.3 73.4 all-reduce.20
  1485.3 73.0 all-reduce.18
  1561.1 31.8 all-reduce.22
  1596.2 59.4 all-gather.10
